TPU v7x, 32 devices: a whole 2x2x4 slice. The times are simulated.
32 devices in a mesh: fsdp: 16 (over z, y, core), ctx: 2 (over x).
Axes of the slice: x: 2, y: 2, z: 4, core: 2. Of those that a mesh axis runs over, the one named last changes fastest.
Arguments:
- q_nope: bfloat16 [16, 256, 1024], P('fsdp', 'ctx'), may hold values from -6 to 6
- q_rope: bfloat16 [16, 256, 512], P('fsdp', 'ctx'), may hold values from -450 to 450
- kv_latent: bfloat16 [16, 256, 512], P('fsdp', 'ctx'), may hold values from -6 to 6
- key_rope: bfloat16 [16, 256, 64], P('fsdp', 'ctx'), may hold values from -6 to 6
- weight_codes: bfloat16 [512, 2048], P('fsdp'), may hold values from -0.25 to 0.25
- exponents: int32 [4, 16], replicated, may hold values from -1 to 1
- doc_ids: int32 [16, 256], P('fsdp'), may hold values from 0 to 3, never falling along the last dimension, each value on 1 to 128 neighbouring positions
Outputs:
- scaled_out: bfloat16 [16, 256, 1024], P('fsdp', 'ctx')
Inputs may be any that keep to these rules, and one draw needn't show every extreme that they name: `doc_ids`: each document of a sequence covers consecutive positions, at most 128 of them.
All inputs are finite; a program needn't handle non-finite values. Where the computation divides by a largest or mean magnitude, that divisor is 1e-20 or more.
Results may differ from a plain program's by a relative error of at most 0.0085.
Values may be sent and summed in bfloat16 or wider, within the bound.
A program may use at most 64 MiB of HBM per device.

v0:
```python
import jax
import jax.numpy as jnp
from jax import lax
from jax.sharding import PartitionSpec as P

DN = 128
DR = 64
DV = 128
BLK = 128


def dequantize(codes, exponents):
    nrow, ncol = exponents.shape
    factor = jnp.exp2(exponents.astype(jnp.float32)).astype(jnp.bfloat16)
    scaled = codes.reshape(nrow, BLK, ncol, BLK) * factor[:, None, :, None]
    return scaled.reshape(codes.shape)


def attend(queries, rotary, keys_values, rope_all, query_places, query_docs, docs):
    length = keys_values.shape[0]
    k_nope = keys_values[:, :, :DN]
    values = keys_values[:, :, DN:]
    scores = jnp.einsum("qhd,khd->hqk", queries, k_nope, preferred_element_type=jnp.float32)
    scores = scores + jnp.einsum(
        "qhd,kd->hqk", rotary, rope_all, preferred_element_type=jnp.float32
    )
    scores = scores * (DN + DR) ** (-0.5)
    key_places = jnp.arange(length, dtype=jnp.int32)
    allowed = (key_places[None, :] <= query_places[:, None]) & (
        docs[None, :] == query_docs[:, None]
    )
    scores = jnp.where(allowed[None], scores, jnp.float32(-1e30))
    top = jnp.max(scores, axis=-1, keepdims=True)
    expo = jnp.exp(scores - top)
    probs = (expo / jnp.sum(expo, axis=-1, keepdims=True)).astype(jnp.bfloat16)
    return jnp.einsum("hqk,khd->qhd", probs, values, preferred_element_type=jnp.float32)


def per_device(q_nope, q_rope, kv_latent, key_rope, weight_codes, exponents, doc_ids):
    tok = q_nope.shape[1]
    heads = q_nope.shape[2] // DN
    groups = lax.axis_size("ctx")
    length = tok * groups
    offset = lax.axis_index("ctx") * tok
    docs = doc_ids[0]
    latent_all, rope_all = (
        lax.all_gather(kv_latent[0], "ctx", axis=0, tiled=True),
        lax.all_gather(key_rope[0], "ctx", axis=0, tiled=True),
    )
    codes = lax.all_gather(weight_codes, "fsdp", axis=0, tiled=True)
    weight = dequantize(codes, exponents)
    keys_values = jnp.dot(latent_all, weight, preferred_element_type=jnp.float32).astype(
        jnp.bfloat16
    )
    keys_values = keys_values.reshape(length, heads, DN + DV)
    queries = q_nope[0].reshape(tok, heads, DN)
    rotary = q_rope[0].reshape(tok, heads, DR)
    query_docs = lax.dynamic_slice_in_dim(docs, offset, tok)
    query_places = offset + jnp.arange(tok, dtype=jnp.int32)
    attended = attend(queries, rotary, keys_values, rope_all, query_places, query_docs, docs)
    attended = attended.reshape(tok, heads * DV)
    amax = lax.pmax(jnp.max(jnp.abs(attended)), ("fsdp", "ctx"))
    return (attended / amax).reshape(1, tok, heads * DV).astype(jnp.bfloat16)


def solution(mesh):
    in_specs = (
        P("fsdp", "ctx", None),
        P("fsdp", "ctx", None),
        P("fsdp", "ctx", None),
        P("fsdp", "ctx", None),
        P("fsdp", None),
        P(),
        P("fsdp", None),
    )
    out_specs = P("fsdp", "ctx", None)
    return jax.shard_map(
        per_device, mesh=mesh, in_specs=in_specs, out_specs=out_specs, check_vma=False
    )
```

profile of v0, /device:TPU:0, one launch (start us, length us, event | category | flops | bytes accessed | tf_op | source)
XLA Modules:
  0.0 105.1 jit_solution(8917940227443522955)
XLA Ops:
  6.5 0.0 all-gather.4.cloned.1.call-start
  6.5 0.7 all-gather.4.cloned.1.call-update
  7.3 1.0 copy.21
  8.3 1.0 copy.15
  9.3 5.6 %all-gather.1 = bf16[1,256,64]{1,2,0:T(8,128)(2,1)S(1)} all-gather(bf16[1,128,64]{1,2,0:T(8,128)(2,1)} %param.10), channel_id=3, replica_groups=mesh['fsdp'=16,'ctx'=2] {'ctx'}, dimensions={1}, use_global_device_ids=true | all-gather | bytes 49152 | tf_op jit(solution)/shard_map/all_gather | solution.py:48
  14.9 5.8 %all-gather = bf16[1,256,512]{2,1,0:T(8,128)(2,1)S(1)} all-gather(bf16[1,128,512]{2,1,0:T(8,128)(2,1)} %param.9), channel_id=2, replica_groups=mesh['fsdp'=16,'ctx'=2] {'ctx'}, dimensions={1}, use_global_device_ids=true | all-gather | bytes 393216 | tf_op jit(solution)/shard_map/all_gather | solution.py:47
  20.8 0.7 dynamic-slice_bitcast_fusion
  21.4 0.7 exponential_convert_fusion
  22.1 0.8 fusion.12
  22.9 30.8 %all-gather.4.cloned.1.call-done = bf16[512,2048]{1,0:T(8,128)(2,1)} async-done(((bf16[32,2048]{1,0:T(8,128)(2,1)}), bf16[512,2048]{1,0:T(8,128)(2,1)}) %all-gather.4.cloned.1.call-update) | async-done | bytes 2097168 | tf_op jit(solution)/shard_map/all_gather | solution.py:50
  53.7 0.0 copy-start
  53.7 0.3 mul.20
  54.1 1.2 %copy-done = bf16[512,2048]{1,0:T(8,128)(2,1)S(1)} copy-done((bf16[512,2048]{1,0:T(8,128)(2,1)S(1)}, bf16[512,2048]{1,0:T(8,128)(2,1)}, u32[]{:S(2)}) %copy-start) | copy-done | bytes 2097176
  55.3 1.2 %convolution_convert_fusion = bf16[2048,256]{1,0:T(8,128)(2,1)S(1)} fusion(bf16[512,2048]{1,0:T(8,128)(2,1)S(1)} %copy-done, bf16[64,8,16,128]{3,2,1,0:T(8,128)(2,1)S(1)} %bitcast.38, bf16[1,256,512]{2,1,0:T(8,128)(2,1)S(1)} %all-gather), kind=kOutput, calls=%fused_computation.1 | convolution fusion | flops 538443776 | bytes 5505024 | tf_op jit(solution)/shard_map/dot_general | solution.py:52
  56.5 0.3 convolution_bitcast_fusion.1
  56.9 0.3 fusion.6
  57.2 0.2 fusion.15
  57.5 1.0 abs_reduce_fusion
  58.5 38.2 %pmax.7 = f32[]{:T(128)} all-reduce(f32[]{:T(128)} %get-tuple-element.5), channel_id=1, replica_groups=mesh['fsdp'=16,'ctx'=2] {'fsdp','ctx'}, use_global_device_ids=true, to_apply=%region_3.4 | all-reduce | flops 1 | bytes 8 | tf_op jit(solution)/shard_map/pmax | solution.py:62
  96.7 0.7 divide_convert_fusion.1
  97.4 0.9 copy.17
  (1 shorter events, 0.0 us)
Async XLA Ops:
  6.5 47.2 %all-gather.4.cloned.1.call-start = ((), (), s32[]{:S(2)}) async-start(), calls=%async_computation | async-start | bytes 2228224 | tf_op jit(solution)/shard_map/all_gather | solution.py:50
  53.7 1.6 %copy-start = (bf16[512,2048]{1,0:T(8,128)(2,1)S(1)}, bf16[512,2048]{1,0:T(8,128)(2,1)}, u32[]{:S(2)}) copy-start(bf16[512,2048]{1,0:T(8,128)(2,1)} %all-gather.4.cloned.1.call-done) | copy-start | bytes 6291460
Sparse Core Ops, SparseCore 0:
  9.5 44.1 all-gather.3
where the time goes:
time: 105 us
  blocking collectives  49.7 us (47%)
  waiting for transfers between devices  31.5 us (30%)
  between operations  13.5 us (13%)
  local copies, waits for them, and re-layouts  5.1 us (5%)
  matrix products  2.96 us (3%)
  other arithmetic  2.4 us (2%)
    pmax x1, blocking collectives, per_device(): amax = lax.pmax(jnp.max(jnp.abs(attended)), ('fsdp', 'ctx'))  38.2 us
    all_gather x1, waiting for transfers between devices, per_device(): codes = lax.all_gather(weight_codes, 'fsdp', axis=0, tiled=True)  30.8 us
    all_gather x1, blocking collectives, per_device(): lax.all_gather(kv_latent[0], 'ctx', axis=0, tiled=True)  5.84 us
    all_gather x1, blocking collectives, per_device(): lax.all_gather(key_rope[0], 'ctx', axis=0, tiled=True)  5.64 us
    unnamed x4, local copies, waits for them, and re-layouts  3.26 us
  transfers between devices with their start and end apart: 1, of which 1 were waited for; matrix products, arithmetic and copies ran while one was open for 4% of the time, Pallas kernels for 0%

commit v1 on v0

--- a/solution.py
+++ b/solution.py
@@ -47,7 +47,12 @@
         lax.all_gather(kv_latent[0], "ctx", axis=0, tiled=True),
         lax.all_gather(key_rope[0], "ctx", axis=0, tiled=True),
     )
-    codes = lax.all_gather(weight_codes, "fsdp", axis=0, tiled=True)
+    ring = [weight_codes]
+    for hop in range(15):
+        ring.append(lax.ppermute(ring[-1], "fsdp", [(dev, (dev + 1) % 16) for dev in range(16)]))
+    codes = jnp.roll(
+        jnp.concatenate(ring[::-1], axis=0), (lax.axis_index("fsdp") + 1) * ring[0].shape[0], axis=0
+    )
     weight = dequantize(codes, exponents)
     keys_values = jnp.dot(latent_all, weight, preferred_element_type=jnp.float32).astype(
         jnp.bfloat16

time: 105 us -> 159 us (1.51); the launches traced: 105 us -> 157 us
  waiting for transfers between devices: 31.5 us -> 98.6 us
  between operations: 13.5 us -> 0.34 us
  blocking collectives: 49.7 us -> 47.5 us
    ppermute x0 -> x15, waiting for transfers between devices: none -> 98.6 us  [per_device(): lax.ppermute(ring[-1], 'fsdp', [(dev, (dev + 1) % 16) for dev in range(16)])]
    all_gather x1 -> x0, waiting for transfers between devices: 30.8 us -> none  [per_device(): codes = lax.all_gather(weight_codes, 'fsdp', axis=0, tiled=True)]
    unnamed x4 -> x35, local copies, waits for them, and re-layouts: 3.26 us -> 2.36 us
  transfers between devices with their start and end apart: 1 -> 15, of which waited for: 1 -> 14; matrix products, arithmetic and copies ran while one was open for 4% -> 3% of each run, Pallas kernels for 0% -> 0%
where the time goes in v1:
time: 159 us; the launch traced here: 157 us
  waiting for transfers between devices  98.6 us (62%)
  blocking collectives  47.5 us (30%)
  local copies, waits for them, and re-layouts  4.22 us (3%)
  matrix products  3.55 us (2%)
  other arithmetic  2.4 us (2%)
    ppermute x15, waiting for transfers between devices, per_device(): lax.ppermute(ring[-1], 'fsdp', [(dev, (dev + 1) % 16) for dev in range(16)])  98.6 us
    pmax x1, blocking collectives, per_device(): amax = lax.pmax(jnp.max(jnp.abs(attended)), ('fsdp', 'ctx'))  37 us
    all_gather x1, blocking collectives, per_device(): lax.all_gather(kv_latent[0], 'ctx', axis=0, tiled=True)  5.84 us
    all_gather x1, blocking collectives, per_device(): lax.all_gather(key_rope[0], 'ctx', axis=0, tiled=True)  4.65 us
  transfers between devices with their start and end apart: 15, of which 14 were waited for; matrix products, arithmetic and copies ran while one was open for 3% of the time, Pallas kernels for 0%

profile of v1, /device:TPU:0, one launch (start us, length us, event | category | flops | bytes accessed | tf_op | source)
XLA Modules:
  0.0 157.1 jit_solution(8313681566779227571)
XLA Ops:
  0.0 0.0 copy-start
  0.0 0.5 collective-permute-start
  0.5 7.9 %collective-permute-done = bf16[32,2048]{1,0:T(8,128)(2,1)S(1)} collective-permute-done((bf16[32,2048]{1,0:T(8,128)(2,1)}, bf16[32,2048]{1,0:T(8,128)(2,1)S(1)}, u32[]{:S(2)}, u32[]{:S(2)}) %collective-permute-start) | collective-permute-done | bytes 131104 | tf_op jit(solution)/shard_map/ppermute | solution.py:52
  8.4 0.0 collective-permute-start.1
  8.4 7.1 %collective-permute-done.1 = bf16[32,2048]{1,0:T(8,128)(2,1)S(1)} collective-permute-done((bf16[32,2048]{1,0:T(8,128)(2,1)S(1)}, bf16[32,2048]{1,0:T(8,128)(2,1)S(1)}, u32[]{:S(2)}, u32[]{:S(2)}) %collective-permute-start.1) | collective-permute-done | bytes 131104 | tf_op jit(solution)/shard_map/ppermute | solution.py:52
  15.5 0.0 collective-permute-start.2
  15.5 7.1 %collective-permute-done.2 = bf16[32,2048]{1,0:T(8,128)(2,1)S(1)} collective-permute-done((bf16[32,2048]{1,0:T(8,128)(2,1)S(1)}, bf16[32,2048]{1,0:T(8,128)(2,1)S(1)}, u32[]{:S(2)}, u32[]{:S(2)}) %collective-permute-start.2) | collective-permute-done | bytes 131104 | tf_op jit(solution)/shard_map/ppermute | solution.py:52
  22.6 0.0 collective-permute-start.3
  22.6 7.1 %collective-permute-done.3 = bf16[32,2048]{1,0:T(8,128)(2,1)S(1)} collective-permute-done((bf16[32,2048]{1,0:T(8,128)(2,1)S(1)}, bf16[32,2048]{1,0:T(8,128)(2,1)S(1)}, u32[]{:S(2)}, u32[]{:S(2)}) %collective-permute-start.3) | collective-permute-done | bytes 131104 | tf_op jit(solution)/shard_map/ppermute | solution.py:52
  29.7 0.0 collective-permute-start.4
  29.7 7.1 %collective-permute-done.4 = bf16[32,2048]{1,0:T(8,128)(2,1)S(1)} collective-permute-done((bf16[32,2048]{1,0:T(8,128)(2,1)S(1)}, bf16[32,2048]{1,0:T(8,128)(2,1)S(1)}, u32[]{:S(2)}, u32[]{:S(2)}) %collective-permute-start.4) | collective-permute-done | bytes 131104 | tf_op jit(solution)/shard_map/ppermute | solution.py:52
  36.8 0.0 collective-permute-start.5
  36.8 7.1 %collective-permute-done.5 = bf16[32,2048]{1,0:T(8,128)(2,1)S(1)} collective-permute-done((bf16[32,2048]{1,0:T(8,128)(2,1)S(1)}, bf16[32,2048]{1,0:T(8,128)(2,1)S(1)}, u32[]{:S(2)}, u32[]{:S(2)}) %collective-permute-start.5) | collective-permute-done | bytes 131104 | tf_op jit(solution)/shard_map/ppermute | solution.py:52
  43.9 0.0 collective-permute-start.6
  43.9 7.1 %collective-permute-done.6 = bf16[32,2048]{1,0:T(8,128)(2,1)S(1)} collective-permute-done((bf16[32,2048]{1,0:T(8,128)(2,1)S(1)}, bf16[32,2048]{1,0:T(8,128)(2,1)S(1)}, u32[]{:S(2)}, u32[]{:S(2)}) %collective-permute-start.6) | collective-permute-done | bytes 131104 | tf_op jit(solution)/shard_map/ppermute | solution.py:52
  51.0 0.0 collective-permute-start.7
  51.0 7.1 %collective-permute-done.7 = bf16[32,2048]{1,0:T(8,128)(2,1)S(1)} collective-permute-done((bf16[32,2048]{1,0:T(8,128)(2,1)S(1)}, bf16[32,2048]{1,0:T(8,128)(2,1)S(1)}, u32[]{:S(2)}, u32[]{:S(2)}) %collective-permute-start.7) | collective-permute-done | bytes 131104 | tf_op jit(solution)/shard_map/ppermute | solution.py:52
  58.0 0.0 collective-permute-start.8
  58.0 7.1 %collective-permute-done.8 = bf16[32,2048]{1,0:T(8,128)(2,1)S(1)} collective-permute-done((bf16[32,2048]{1,0:T(8,128)(2,1)S(1)}, bf16[32,2048]{1,0:T(8,128)(2,1)S(1)}, u32[]{:S(2)}, u32[]{:S(2)}) %collective-permute-start.8) | collective-permute-done | bytes 131104 | tf_op jit(solution)/shard_map/ppermute | solution.py:52
  65.1 0.0 collective-permute-start.9
  65.1 7.1 %collective-permute-done.9 = bf16[32,2048]{1,0:T(8,128)(2,1)S(1)} collective-permute-done((bf16[32,2048]{1,0:T(8,128)(2,1)S(1)}, bf16[32,2048]{1,0:T(8,128)(2,1)S(1)}, u32[]{:S(2)}, u32[]{:S(2)}) %collective-permute-start.9) | collective-permute-done | bytes 131104 | tf_op jit(solution)/shard_map/ppermute | solution.py:52
  72.2 0.0 collective-permute-start.10
  72.2 7.1 %collective-permute-done.10 = bf16[32,2048]{1,0:T(8,128)(2,1)S(1)} collective-permute-done((bf16[32,2048]{1,0:T(8,128)(2,1)S(1)}, bf16[32,2048]{1,0:T(8,128)(2,1)S(1)}, u32[]{:S(2)}, u32[]{:S(2)}) %collective-permute-start.10) | collective-permute-done | bytes 131104 | tf_op jit(solution)/shard_map/ppermute | solution.py:52
  79.3 0.0 collective-permute-start.11
  79.3 7.1 %collective-permute-done.11 = bf16[32,2048]{1,0:T(8,128)(2,1)S(1)} collective-permute-done((bf16[32,2048]{1,0:T(8,128)(2,1)S(1)}, bf16[32,2048]{1,0:T(8,128)(2,1)S(1)}, u32[]{:S(2)}, u32[]{:S(2)}) %collective-permute-start.11) | collective-permute-done | bytes 131104 | tf_op jit(solution)/shard_map/ppermute | solution.py:52
  86.4 0.0 collective-permute-start.12
  86.4 0.7 dynamic-slice_bitcast_fusion
  87.1 6.4 %collective-permute-done.12 = bf16[32,2048]{1,0:T(8,128)(2,1)S(1)} collective-permute-done((bf16[32,2048]{1,0:T(8,128)(2,1)S(1)}, bf16[32,2048]{1,0:T(8,128)(2,1)S(1)}, u32[]{:S(2)}, u32[]{:S(2)}) %collective-permute-start.12) | collective-permute-done | bytes 131104 | tf_op jit(solution)/shard_map/ppermute | solution.py:52
  93.5 0.0 collective-permute-start.13
  93.5 0.8 fusion.13
  94.3 6.3 %collective-permute-done.13 = bf16[32,2048]{1,0:T(8,128)(2,1)S(1)} collective-permute-done((bf16[32,2048]{1,0:T(8,128)(2,1)S(1)}, bf16[32,2048]{1,0:T(8,128)(2,1)S(1)}, u32[]{:S(2)}, u32[]{:S(2)}) %collective-permute-start.13) | collective-permute-done | bytes 131104 | tf_op jit(solution)/shard_map/ppermute | solution.py:52
  100.6 0.0 collective-permute-start.14
  100.6 0.7 exponential_convert_fusion
  101.3 1.0 copy.21
  102.3 1.0 copy.15
  103.3 4.6 %all-gather.1 = bf16[1,256,64]{1,2,0:T(8,128)(2,1)S(1)} all-gather(bf16[1,128,64]{1,2,0:T(8,128)(2,1)} %param.10), channel_id=3, replica_groups=mesh['fsdp'=16,'ctx'=2] {'ctx'}, dimensions={1}, use_global_device_ids=true | all-gather | bytes 49152 | tf_op jit(solution)/shard_map/all_gather | solution.py:48
  108.0 5.8 %all-gather = bf16[1,256,512]{2,1,0:T(8,128)(2,1)S(1)} all-gather(bf16[1,128,512]{2,1,0:T(8,128)(2,1)} %param.9), channel_id=2, replica_groups=mesh['fsdp'=16,'ctx'=2] {'ctx'}, dimensions={1}, use_global_device_ids=true | all-gather | bytes 393216 | tf_op jit(solution)/shard_map/all_gather | solution.py:47
  113.8 0.0 collective-permute-done.14
  114.1 0.0 copy-done
  114.4 0.3 mul.24
  114.8 1.8 %convolution_convert_fusion = bf16[2048,256]{1,0:T(8,128)(2,1)S(1)} fusion(bf16[64,8,16,128]{3,2,1,0:T(8,128)(2,1)S(1)} %bitcast.38, bf16[1024,2048]{1,0:T(8,128)(2,1)S(1)} %constant_dynamic-update-slice_fusion, s32[]{:T(128)S(6)} %select_n.21, bf16[1,256,512]{2,1,0:T(8,128)(2,1)S(1)} %all-gather), kind=kOutput, calls=%fused_computation.1 | convolution fusion | flops 541589504 | bytes 5505028 | tf_op jit(solution)/shard_map/dot_general | solution.py:57
  116.6 0.3 convolution_bitcast_fusion.1
  116.9 0.3 fusion.7
  117.3 0.2 fusion.17
  117.5 1.0 abs_reduce_fusion
  118.6 37.0 %pmax.7 = f32[]{:T(128)} all-reduce(f32[]{:T(128)} %get-tuple-element.5), channel_id=1, replica_groups=mesh['fsdp'=16,'ctx'=2] {'fsdp','ctx'}, use_global_device_ids=true, to_apply=%region_3.4 | all-reduce | flops 1 | bytes 8 | tf_op jit(solution)/shard_map/pmax | solution.py:67
  155.6 0.7 divide_convert_fusion.1
  156.3 0.9 copy.17
  (33 shorter events, 0.4 us)
Async XLA Ops:
  0.0 114.1 %copy-start = (bf16[32,2048]{1,0:T(8,128)(2,1)S(1)}, bf16[32,2048]{1,0:T(8,128)(2,1)}, u32[]{:S(2)}) copy-start(bf16[32,2048]{1,0:T(8,128)(2,1)} %param.11) | copy-start | bytes 393220
  0.0 8.4 %collective-permute-start = (bf16[32,2048]{1,0:T(8,128)(2,1)}, bf16[32,2048]{1,0:T(8,128)(2,1)S(1)}, u32[]{:S(2)}, u32[]{:S(2)}) collective-permute-start(bf16[32,2048]{1,0:T(8,128)(2,1)} %param.11), channel_id=1, source_target_pairs={{0,2},{2,4},{4,6},{6,8},{8,10},{10,12},{12,14},{14,16},{16,18},{18... | collective-permute-start | bytes 393224 | tf_op jit(solution)/shard_map/ppermute | solution.py:52
  8.4 7.1 %collective-permute-start.1 = (bf16[32,2048]{1,0:T(8,128)(2,1)S(1)}, bf16[32,2048]{1,0:T(8,128)(2,1)S(1)}, u32[]{:S(2)}, u32[]{:S(2)}) collective-permute-start(bf16[32,2048]{1,0:T(8,128)(2,1)S(1)} %collective-permute-done), channel_id=1, source_target_pairs={{0,2},{2,4},{4,6},{6,8},{8,10},{10,12},{12,14},{14,16},{16,18},{18... | collective-permute-start | bytes 393224 | tf_op jit(solution)/shard_map/ppermute | solution.py:52
  15.5 7.1 %collective-permute-start.2 = (bf16[32,2048]{1,0:T(8,128)(2,1)S(1)}, bf16[32,2048]{1,0:T(8,128)(2,1)S(1)}, u32[]{:S(2)}, u32[]{:S(2)}) collective-permute-start(bf16[32,2048]{1,0:T(8,128)(2,1)S(1)} %collective-permute-done.1), channel_id=1, source_target_pairs={{0,2},{2,4},{4,6},{6,8},{8,10},{10,12},{12,14},{14,16},{16,18},{18... | collective-permute-start | bytes 393224 | tf_op jit(solution)/shard_map/ppermute | solution.py:52
  22.6 7.1 %collective-permute-start.3 = (bf16[32,2048]{1,0:T(8,128)(2,1)S(1)}, bf16[32,2048]{1,0:T(8,128)(2,1)S(1)}, u32[]{:S(2)}, u32[]{:S(2)}) collective-permute-start(bf16[32,2048]{1,0:T(8,128)(2,1)S(1)} %collective-permute-done.2), channel_id=1, source_target_pairs={{0,2},{2,4},{4,6},{6,8},{8,10},{10,12},{12,14},{14,16},{16,18},{18... | collective-permute-start | bytes 393224 | tf_op jit(solution)/shard_map/ppermute | solution.py:52
  29.7 7.1 %collective-permute-start.4 = (bf16[32,2048]{1,0:T(8,128)(2,1)S(1)}, bf16[32,2048]{1,0:T(8,128)(2,1)S(1)}, u32[]{:S(2)}, u32[]{:S(2)}) collective-permute-start(bf16[32,2048]{1,0:T(8,128)(2,1)S(1)} %collective-permute-done.3), channel_id=1, source_target_pairs={{0,2},{2,4},{4,6},{6,8},{8,10},{10,12},{12,14},{14,16},{16,18},{18... | collective-permute-start | bytes 393224 | tf_op jit(solution)/shard_map/ppermute | solution.py:52
  36.8 7.1 %collective-permute-start.5 = (bf16[32,2048]{1,0:T(8,128)(2,1)S(1)}, bf16[32,2048]{1,0:T(8,128)(2,1)S(1)}, u32[]{:S(2)}, u32[]{:S(2)}) collective-permute-start(bf16[32,2048]{1,0:T(8,128)(2,1)S(1)} %collective-permute-done.4), channel_id=1, source_target_pairs={{0,2},{2,4},{4,6},{6,8},{8,10},{10,12},{12,14},{14,16},{16,18},{18... | collective-permute-start | bytes 393224 | tf_op jit(solution)/shard_map/ppermute | solution.py:52
  43.9 7.1 %collective-permute-start.6 = (bf16[32,2048]{1,0:T(8,128)(2,1)S(1)}, bf16[32,2048]{1,0:T(8,128)(2,1)S(1)}, u32[]{:S(2)}, u32[]{:S(2)}) collective-permute-start(bf16[32,2048]{1,0:T(8,128)(2,1)S(1)} %collective-permute-done.5), channel_id=1, source_target_pairs={{0,2},{2,4},{4,6},{6,8},{8,10},{10,12},{12,14},{14,16},{16,18},{18... | collective-permute-start | bytes 393224 | tf_op jit(solution)/shard_map/ppermute | solution.py:52
  51.0 7.1 %collective-permute-start.7 = (bf16[32,2048]{1,0:T(8,128)(2,1)S(1)}, bf16[32,2048]{1,0:T(8,128)(2,1)S(1)}, u32[]{:S(2)}, u32[]{:S(2)}) collective-permute-start(bf16[32,2048]{1,0:T(8,128)(2,1)S(1)} %collective-permute-done.6), channel_id=1, source_target_pairs={{0,2},{2,4},{4,6},{6,8},{8,10},{10,12},{12,14},{14,16},{16,18},{18... | collective-permute-start | bytes 393224 | tf_op jit(solution)/shard_map/ppermute | solution.py:52
  58.0 7.1 %collective-permute-start.8 = (bf16[32,2048]{1,0:T(8,128)(2,1)S(1)}, bf16[32,2048]{1,0:T(8,128)(2,1)S(1)}, u32[]{:S(2)}, u32[]{:S(2)}) collective-permute-start(bf16[32,2048]{1,0:T(8,128)(2,1)S(1)} %collective-permute-done.7), channel_id=1, source_target_pairs={{0,2},{2,4},{4,6},{6,8},{8,10},{10,12},{12,14},{14,16},{16,18},{18... | collective-permute-start | bytes 393224 | tf_op jit(solution)/shard_map/ppermute | solution.py:52
  65.1 7.1 %collective-permute-start.9 = (bf16[32,2048]{1,0:T(8,128)(2,1)S(1)}, bf16[32,2048]{1,0:T(8,128)(2,1)S(1)}, u32[]{:S(2)}, u32[]{:S(2)}) collective-permute-start(bf16[32,2048]{1,0:T(8,128)(2,1)S(1)} %collective-permute-done.8), channel_id=1, source_target_pairs={{0,2},{2,4},{4,6},{6,8},{8,10},{10,12},{12,14},{14,16},{16,18},{18... | collective-permute-start | bytes 393224 | tf_op jit(solution)/shard_map/ppermute | solution.py:52
  72.2 7.1 %collective-permute-start.10 = (bf16[32,2048]{1,0:T(8,128)(2,1)S(1)}, bf16[32,2048]{1,0:T(8,128)(2,1)S(1)}, u32[]{:S(2)}, u32[]{:S(2)}) collective-permute-start(bf16[32,2048]{1,0:T(8,128)(2,1)S(1)} %collective-permute-done.9), channel_id=1, source_target_pairs={{0,2},{2,4},{4,6},{6,8},{8,10},{10,12},{12,14},{14,16},{16,18},{18... | collective-permute-start | bytes 393224 | tf_op jit(solution)/shard_map/ppermute | solution.py:52
  79.3 7.1 %collective-permute-start.11 = (bf16[32,2048]{1,0:T(8,128)(2,1)S(1)}, bf16[32,2048]{1,0:T(8,128)(2,1)S(1)}, u32[]{:S(2)}, u32[]{:S(2)}) collective-permute-start(bf16[32,2048]{1,0:T(8,128)(2,1)S(1)} %collective-permute-done.10), channel_id=1, source_target_pairs={{0,2},{2,4},{4,6},{6,8},{8,10},{10,12},{12,14},{14,16},{16,18},{18... | collective-permute-start | bytes 393224 | tf_op jit(solution)/shard_map/ppermute | solution.py:52
  86.4 7.1 %collective-permute-start.12 = (bf16[32,2048]{1,0:T(8,128)(2,1)S(1)}, bf16[32,2048]{1,0:T(8,128)(2,1)S(1)}, u32[]{:S(2)}, u32[]{:S(2)}) collective-permute-start(bf16[32,2048]{1,0:T(8,128)(2,1)S(1)} %collective-permute-done.11), channel_id=1, source_target_pairs={{0,2},{2,4},{4,6},{6,8},{8,10},{10,12},{12,14},{14,16},{16,18},{18... | collective-permute-start | bytes 393224 | tf_op jit(solution)/shard_map/ppermute | solution.py:52
  93.5 7.1 %collective-permute-start.13 = (bf16[32,2048]{1,0:T(8,128)(2,1)S(1)}, bf16[32,2048]{1,0:T(8,128)(2,1)S(1)}, u32[]{:S(2)}, u32[]{:S(2)}) collective-permute-start(bf16[32,2048]{1,0:T(8,128)(2,1)S(1)} %collective-permute-done.12), channel_id=1, source_target_pairs={{0,2},{2,4},{4,6},{6,8},{8,10},{10,12},{12,14},{14,16},{16,18},{18... | collective-permute-start | bytes 393224 | tf_op jit(solution)/shard_map/ppermute | solution.py:52
  100.6 13.2 %collective-permute-start.14 = (bf16[32,2048]{1,0:T(8,128)(2,1)S(1)}, bf16[32,2048]{1,0:T(8,128)(2,1)S(1)}, u32[]{:S(2)}, u32[]{:S(2)}) collective-permute-start(bf16[32,2048]{1,0:T(8,128)(2,1)S(1)} %collective-permute-done.13), channel_id=1, source_target_pairs={{0,2},{2,4},{4,6},{6,8},{8,10},{10,12},{12,14},{14,16},{16,18},{18... | collective-permute-start | bytes 393224 | tf_op jit(solution)/shard_map/ppermute | solution.py:52
